TPU v7x, 256 devices: a whole 4x4x8 slice. The times are simulated.
256 devices in a mesh: seq: 32 (over z, x), blk: 8 (over y, core).
Axes of the slice: x: 4, y: 4, z: 8, core: 2. Of those that a mesh axis runs over, the one named last changes fastest.
Arguments:
- qkv: bfloat16 [32768, 12288], P(('seq', 'blk')), may hold values from -24 to 24
- kept_kv: bfloat16 [32, 2, 128, 4096], P('blk', None, None, 'seq'), may hold values from -24 to 24
- cur_list: int32 [256, 8], replicated, may hold values from 0 to 255, as said below
- kept_list: int32 [256, 12], replicated, may hold values from 0 to 31, as said below
- kept_count: int32 [256], replicated, may hold values from 1 to 12, as said below
Outputs:
- attn_out: bfloat16 [32768, 4096], P(('seq', 'blk'))
Inputs may be any that keep to these rules, and one draw needn't show every extreme that they name: `cur_list`: row t lists 8 different tiles t2 of tile t's spatial region, that is with (t2) % 8 equal to (t) % 8; the first entry is t itself. `kept_list`: each row names 12 different kept blocks. `kept_count`: some tile uses all 12 slots.
All inputs are finite; a program needn't handle non-finite values.
Results may differ from a plain program's by a relative error of at most 0.0025.
Values may be sent and summed in bfloat16 or wider, within the bound.
A program may use at most 64 MiB of HBM per device.

v0:
```python
import math
import jax
import jax.numpy as jnp
from jax import lax
from jax.sharding import PartitionSpec as P

HEAD_DIM = 128
MASKED_SCORE = -1e30


def per_device(qkv, kept_kv, cur_list, kept_list, kept_count):
    seq_count = lax.axis_size("seq")
    blk_count = lax.axis_size("blk")
    tok_rows = qkv.shape[0]
    head_width = HEAD_DIM
    head_total = qkv.shape[1] // (3 * head_width)
    tile_len = kept_kv.shape[2]
    tiles_dev = tok_rows // tile_len
    shaped = qkv.reshape(tok_rows, 3, head_total, head_width)
    arrived = lax.all_to_all(shaped, "seq", split_axis=2, concat_axis=0, tiled=True)
    head_dev = arrived.shape[2]
    tile_mine = seq_count * tiles_dev
    grouped = arrived.reshape(tile_mine, tile_len, 3, head_dev, head_width)
    ordered = jnp.transpose(grouped, (2, 0, 3, 1, 4))
    queries_all = ordered[0]
    near_keys_all = ordered[1]
    near_values_all = ordered[2]
    kept_all = lax.all_gather(kept_kv, "blk", axis=0, tiled=True)
    kept_all = jnp.transpose(
        kept_all.reshape(kept_all.shape[0], 2, tile_len, head_dev, head_width), (0, 1, 3, 2, 4)
    )
    far_keys_all = kept_all[:, 0]
    far_values_all = kept_all[:, 1]
    region = lax.axis_index("blk")
    local_ids = jnp.arange(tile_mine, dtype=jnp.int32)
    tile_ids = (local_ids // tiles_dev * blk_count + region) * tiles_dev + local_ids % tiles_dev
    cur_ids = cur_list[tile_ids]
    cur_local = cur_ids // tiles_dev // blk_count * tiles_dev + cur_ids % tiles_dev
    kept_ids = kept_list[tile_ids]
    slot_counts = kept_count[tile_ids]
    score_scale = 1.0 / math.sqrt(head_width)
    window_slots = kept_ids.shape[1]
    near_count = cur_local.shape[1]
    tiles_step = 4
    step_total = tile_mine // tiles_step

    def attend(pieces):
        queries, cur_sel, kept_sel, slot_count = pieces
        near_keys = near_keys_all[cur_sel]
        near_values = near_values_all[cur_sel]
        near_scores = (
            jnp.einsum("bhid,bnhkd->bhink", queries, near_keys, preferred_element_type=jnp.float32)
            * score_scale
        )
        near_max = near_scores.max(axis=(3, 4))[..., None, None]
        far_keys = far_keys_all[kept_sel]
        far_values = far_values_all[kept_sel]
        far_scores = (
            jnp.einsum("bhid,bwhkd->bhiwk", queries, far_keys, preferred_element_type=jnp.float32)
            * score_scale
        )
        is_live = (jnp.arange(window_slots)[None, :] < slot_count[:, None])[:, None, None, :, None]
        far_scores = jnp.where(is_live, far_scores, MASKED_SCORE)
        row_max = jnp.maximum(near_max, far_scores.max(axis=(3, 4))[..., None, None])
        near_weights = jnp.exp(near_scores - row_max)
        far_weights = jnp.where(is_live, jnp.exp(far_scores - row_max), 0.0)
        row_total = near_weights.sum(axis=(3, 4)) + far_weights.sum(axis=(3, 4))
        mixture = jnp.einsum(
            "bhink,bnhkd->bhid",
            near_weights.astype(jnp.bfloat16),
            near_values,
            preferred_element_type=jnp.float32,
        )
        mixture = mixture + jnp.einsum(
            "bhiwk,bwhkd->bhid",
            far_weights.astype(jnp.bfloat16),
            far_values,
            preferred_element_type=jnp.float32,
        )
        result_rows = (mixture / row_total[..., None]).astype(jnp.bfloat16)
        return jnp.transpose(result_rows, (0, 2, 1, 3))

    attended = lax.map(
        attend,
        (
            queries_all.reshape(step_total, tiles_step, head_dev, tile_len, head_width),
            cur_local.reshape(step_total, tiles_step, near_count),
            kept_ids.reshape(step_total, tiles_step, window_slots),
            slot_counts.reshape(step_total, tiles_step),
        ),
    )
    attended = attended.reshape(seq_count * tok_rows, head_dev, head_width)
    returned = lax.all_to_all(attended, "seq", split_axis=0, concat_axis=1, tiled=True)
    return returned.reshape(tok_rows, head_total * head_width)


def solution(mesh):
    placed = (P(("seq", "blk"), None), P("blk", None, None, "seq"), P(), P(), P())
    return jax.shard_map(
        per_device, mesh=mesh, in_specs=placed, out_specs=P(("seq", "blk"), None), check_vma=False
    )
```

profile of v0, /device:TPU:2, one launch (start us, length us, event | category | flops | bytes accessed | tf_op | source)
XLA Modules:
  0.0 308.9 jit_solution(16223919463636740690)
XLA Ops:
  6.5 3.5 %copy.45 = bf16[128,12288]{0,1:T(8,128)(2,1)S(1)} copy(bf16[128,12288]{1,0:T(8,128)(2,1)} %param.7) | data formatting | bytes 6291456 | tf_op args[0]
  11.9 11.7 %all-to-all-start = ((bf16[128,3,32,128]{0,3,1,2:T(8,128)(2,1)}), bf16[128,3,32,128]{0,3,1,2:T(8,128)(2,1)S(1)}, u32[]{:S(2)}, u32[]{:S(2)}) async-start(bf16[128,3,32,128]{0,3,1,2:T(8,128)(2,1)} %copy.46), calls=%async_computation | async-start | bytes 6291456 | tf_op jit(solution)/shard_map/all_to_all | solution.py:20
  26.8 28.6 %all-gather.2.cloned.1.call-done = bf16[32,2,128,128]{3,2,0,1:T(8,128)(2,1)} async-done(((bf16[4,2,128,128]{3,2,0,1:T(8,128)(2,1)}), bf16[32,2,128,128]{3,2,0,1:T(8,128)(2,1)}) %all-gather.2.cloned.1.call-update) | async-done | bytes 2097168 | tf_op jit(solution)/shard_map/all_gather | solution.py:28
  55.4 3.1 %slice_bitcast_fusion = (bf16[32,1,128,128]{3,2,1,0:T(8,128)(2,1)}, bf16[32,1,128,128]{3,2,1,0:T(8,128)(2,1)}) fusion(bf16[32,2,1,128,128]{4,3,0,2,1:T(8,128)(2,1)} %bitcast.130), kind=kLoop, calls=%fused_computation.46 | loop fusion | bytes 4194304 | tf_op jit(solution)/shard_map/squeeze | solution.py:33
  58.5 36.5 %all-to-all-done = bf16[128,3,32,128]{0,3,1,2:T(8,128)(2,1)S(1)} async-done(((bf16[128,3,32,128]{0,3,1,2:T(8,128)(2,1)}), bf16[128,3,32,128]{0,3,1,2:T(8,128)(2,1)S(1)}, u32[]{:S(2)}, u32[]{:S(2)}) %all-to-all-start) | async-done | bytes 3145760 | tf_op jit(solution)/shard_map/all_to_all | solution.py:20
  96.7 2.3 copy.51
  100.3 160.1 %while.10 = (s32[]{:T(128)}, bf16[8,4,128,1,128]{4,2,1,3,0:T(8,128)(2,1)}, bf16[8,4,1,128,128]{3,4,1,0,2:T(8,128)(2,1)}, s32[8,4,8]{2,1,0:T(4,128)S(1)}, bf16[32...) while((s32[]{:T(128)}, ...), condition=%wide.region_5.6_spmd, body=%wide.region_0.5_spmd.sunk | while | flops 685704448 | bytes 57583712 | solution.py:83
  100.4 2.1 gather_fusion.2
  102.6 3.1 %fusion.67 = (f32[4,128]{1,0:T(4,128)S(1)}, f32[4,128,12,128]{1,3,2,0:T(8,128)}) fusion(pred[4,12]{1,0:T(4,128)(4,1)S(1)} %iota_compare_fusion.2, bf16[4,12,128,128]{3,2,1,0:T(8,128)(2,1)S(1)} %bitcast.120, bf16[8,4,1,128,128]{3,4,1,0,2:T(8,128)(2,1)} %get-tuple-element.220, s32[]{:T(128)} %get-tuple-element.207), kind=kOutput, calls=%fused_computation.9.clone.1 | convolution fusion | flops 203685376 | bytes 4852272 | tf_op jit(solution)/shard_map/while/body/eval_jaxpr/bhid,bwhkd->bhiwk/dot_general | solution.py:59
  111.1 2.0 gather_fusion
  113.7 3.4 %gather_fusion.3 = bf16[48,128,128]{2,1,0:T(8,128)(2,1)} fusion(bf16[32,128,128]{2,1,0:T(8,128)(2,1)} %bitcast.123, s32[1024]{0:T(1024)S(1)} %pad_clamp_fusion.6), kind=kCustom, calls=%fused_computation.3.clone.1 | custom fusion | bytes 3145920 | tf_op jit(solution)/shard_map/while/body/eval_jaxpr/gather | solution.py:57
  117.1 3.2 %fusion.70 = bf16[8,4,128,1,128]{4,2,1,3,0:T(8,128)(2,1)} fusion(bf16[8,4,128,1,128]{4,2,1,3,0:T(8,128)(2,1)} %get-tuple-element.208, s32[]{:T(128)} %get-tuple-element.207, f32[4,128,128]{2,1,0:T(8,128)S(1)} %convolution_bitcast_fusion.2, bf16[4,12,128,128]{3,2,1,0:T(8,128)(2,1)} %bitcast.124, f32[4,128,12,128]{1,3,2,0:T(8,128)S(1)} %copy-done.2, ...), kind=kOutput, calls=%fused_computation.24.clone.1 | convolution fusion | flops 205455360 | bytes 5116464 | tf_op jit(solution)/shard_map/while/body/eval_jaxpr/bhiwk,bwhkd->bhid/dot_general | solution.py:74
  120.4 2.1 gather_fusion.2
  122.6 3.1 %fusion.67 = (f32[4,128]{1,0:T(4,128)S(1)}, f32[4,128,12,128]{1,3,2,0:T(8,128)}) fusion(pred[4,12]{1,0:T(4,128)(4,1)S(1)} %iota_compare_fusion.2, bf16[4,12,128,128]{3,2,1,0:T(8,128)(2,1)S(1)} %bitcast.120, bf16[8,4,1,128,128]{3,4,1,0,2:T(8,128)(2,1)} %get-tuple-element.220, s32[]{:T(128)} %get-tuple-element.207), kind=kOutput, calls=%fused_computation.9.clone.1 | convolution fusion | flops 203685376 | bytes 4852272 | tf_op jit(solution)/shard_map/while/body/eval_jaxpr/bhid,bwhkd->bhiwk/dot_general | solution.py:59
  131.1 2.0 gather_fusion
  133.7 3.4 %gather_fusion.3 = bf16[48,128,128]{2,1,0:T(8,128)(2,1)} fusion(bf16[32,128,128]{2,1,0:T(8,128)(2,1)} %bitcast.123, s32[1024]{0:T(1024)S(1)} %pad_clamp_fusion.6), kind=kCustom, calls=%fused_computation.3.clone.1 | custom fusion | bytes 3145920 | tf_op jit(solution)/shard_map/while/body/eval_jaxpr/gather | solution.py:57
  137.1 3.2 %fusion.70 = bf16[8,4,128,1,128]{4,2,1,3,0:T(8,128)(2,1)} fusion(bf16[8,4,128,1,128]{4,2,1,3,0:T(8,128)(2,1)} %get-tuple-element.208, s32[]{:T(128)} %get-tuple-element.207, f32[4,128,128]{2,1,0:T(8,128)S(1)} %convolution_bitcast_fusion.2, bf16[4,12,128,128]{3,2,1,0:T(8,128)(2,1)} %bitcast.124, f32[4,128,12,128]{1,3,2,0:T(8,128)S(1)} %copy-done.2, ...), kind=kOutput, calls=%fused_computation.24.clone.1 | convolution fusion | flops 205455360 | bytes 5116464 | tf_op jit(solution)/shard_map/while/body/eval_jaxpr/bhiwk,bwhkd->bhid/dot_general | solution.py:74
  140.5 2.1 gather_fusion.2
  142.6 3.1 %fusion.67 = (f32[4,128]{1,0:T(4,128)S(1)}, f32[4,128,12,128]{1,3,2,0:T(8,128)}) fusion(pred[4,12]{1,0:T(4,128)(4,1)S(1)} %iota_compare_fusion.2, bf16[4,12,128,128]{3,2,1,0:T(8,128)(2,1)S(1)} %bitcast.120, bf16[8,4,1,128,128]{3,4,1,0,2:T(8,128)(2,1)} %get-tuple-element.220, s32[]{:T(128)} %get-tuple-element.207), kind=kOutput, calls=%fused_computation.9.clone.1 | convolution fusion | flops 203685376 | bytes 4852272 | tf_op jit(solution)/shard_map/while/body/eval_jaxpr/bhid,bwhkd->bhiwk/dot_general | solution.py:59
  151.1 2.0 gather_fusion
  153.7 3.4 %gather_fusion.3 = bf16[48,128,128]{2,1,0:T(8,128)(2,1)} fusion(bf16[32,128,128]{2,1,0:T(8,128)(2,1)} %bitcast.123, s32[1024]{0:T(1024)S(1)} %pad_clamp_fusion.6), kind=kCustom, calls=%fused_computation.3.clone.1 | custom fusion | bytes 3145920 | tf_op jit(solution)/shard_map/while/body/eval_jaxpr/gather | solution.py:57
  157.1 3.2 %fusion.70 = bf16[8,4,128,1,128]{4,2,1,3,0:T(8,128)(2,1)} fusion(bf16[8,4,128,1,128]{4,2,1,3,0:T(8,128)(2,1)} %get-tuple-element.208, s32[]{:T(128)} %get-tuple-element.207, f32[4,128,128]{2,1,0:T(8,128)S(1)} %convolution_bitcast_fusion.2, bf16[4,12,128,128]{3,2,1,0:T(8,128)(2,1)} %bitcast.124, f32[4,128,12,128]{1,3,2,0:T(8,128)S(1)} %copy-done.2, ...), kind=kOutput, calls=%fused_computation.24.clone.1 | convolution fusion | flops 205455360 | bytes 5116464 | tf_op jit(solution)/shard_map/while/body/eval_jaxpr/bhiwk,bwhkd->bhid/dot_general | solution.py:74
  160.5 2.1 gather_fusion.2
  162.7 3.1 %fusion.67 = (f32[4,128]{1,0:T(4,128)S(1)}, f32[4,128,12,128]{1,3,2,0:T(8,128)}) fusion(pred[4,12]{1,0:T(4,128)(4,1)S(1)} %iota_compare_fusion.2, bf16[4,12,128,128]{3,2,1,0:T(8,128)(2,1)S(1)} %bitcast.120, bf16[8,4,1,128,128]{3,4,1,0,2:T(8,128)(2,1)} %get-tuple-element.220, s32[]{:T(128)} %get-tuple-element.207), kind=kOutput, calls=%fused_computation.9.clone.1 | convolution fusion | flops 203685376 | bytes 4852272 | tf_op jit(solution)/shard_map/while/body/eval_jaxpr/bhid,bwhkd->bhiwk/dot_general | solution.py:59
  171.1 2.0 gather_fusion
  173.7 3.4 %gather_fusion.3 = bf16[48,128,128]{2,1,0:T(8,128)(2,1)} fusion(bf16[32,128,128]{2,1,0:T(8,128)(2,1)} %bitcast.123, s32[1024]{0:T(1024)S(1)} %pad_clamp_fusion.6), kind=kCustom, calls=%fused_computation.3.clone.1 | custom fusion | bytes 3145920 | tf_op jit(solution)/shard_map/while/body/eval_jaxpr/gather | solution.py:57
  177.2 3.2 %fusion.70 = bf16[8,4,128,1,128]{4,2,1,3,0:T(8,128)(2,1)} fusion(bf16[8,4,128,1,128]{4,2,1,3,0:T(8,128)(2,1)} %get-tuple-element.208, s32[]{:T(128)} %get-tuple-element.207, f32[4,128,128]{2,1,0:T(8,128)S(1)} %convolution_bitcast_fusion.2, bf16[4,12,128,128]{3,2,1,0:T(8,128)(2,1)} %bitcast.124, f32[4,128,12,128]{1,3,2,0:T(8,128)S(1)} %copy-done.2, ...), kind=kOutput, calls=%fused_computation.24.clone.1 | convolution fusion | flops 205455360 | bytes 5116464 | tf_op jit(solution)/shard_map/while/body/eval_jaxpr/bhiwk,bwhkd->bhid/dot_general | solution.py:74
  180.5 2.1 gather_fusion.2
  182.7 3.1 %fusion.67 = (f32[4,128]{1,0:T(4,128)S(1)}, f32[4,128,12,128]{1,3,2,0:T(8,128)}) fusion(pred[4,12]{1,0:T(4,128)(4,1)S(1)} %iota_compare_fusion.2, bf16[4,12,128,128]{3,2,1,0:T(8,128)(2,1)S(1)} %bitcast.120, bf16[8,4,1,128,128]{3,4,1,0,2:T(8,128)(2,1)} %get-tuple-element.220, s32[]{:T(128)} %get-tuple-element.207), kind=kOutput, calls=%fused_computation.9.clone.1 | convolution fusion | flops 203685376 | bytes 4852272 | tf_op jit(solution)/shard_map/while/body/eval_jaxpr/bhid,bwhkd->bhiwk/dot_general | solution.py:59
  191.2 2.0 gather_fusion
  193.8 3.4 %gather_fusion.3 = bf16[48,128,128]{2,1,0:T(8,128)(2,1)} fusion(bf16[32,128,128]{2,1,0:T(8,128)(2,1)} %bitcast.123, s32[1024]{0:T(1024)S(1)} %pad_clamp_fusion.6), kind=kCustom, calls=%fused_computation.3.clone.1 | custom fusion | bytes 3145920 | tf_op jit(solution)/shard_map/while/body/eval_jaxpr/gather | solution.py:57
  197.2 3.2 %fusion.70 = bf16[8,4,128,1,128]{4,2,1,3,0:T(8,128)(2,1)} fusion(bf16[8,4,128,1,128]{4,2,1,3,0:T(8,128)(2,1)} %get-tuple-element.208, s32[]{:T(128)} %get-tuple-element.207, f32[4,128,128]{2,1,0:T(8,128)S(1)} %convolution_bitcast_fusion.2, bf16[4,12,128,128]{3,2,1,0:T(8,128)(2,1)} %bitcast.124, f32[4,128,12,128]{1,3,2,0:T(8,128)S(1)} %copy-done.2, ...), kind=kOutput, calls=%fused_computation.24.clone.1 | convolution fusion | flops 205455360 | bytes 5116464 | tf_op jit(solution)/shard_map/while/body/eval_jaxpr/bhiwk,bwhkd->bhid/dot_general | solution.py:74
  200.5 2.1 gather_fusion.2
  202.7 3.1 %fusion.67 = (f32[4,128]{1,0:T(4,128)S(1)}, f32[4,128,12,128]{1,3,2,0:T(8,128)}) fusion(pred[4,12]{1,0:T(4,128)(4,1)S(1)} %iota_compare_fusion.2, bf16[4,12,128,128]{3,2,1,0:T(8,128)(2,1)S(1)} %bitcast.120, bf16[8,4,1,128,128]{3,4,1,0,2:T(8,128)(2,1)} %get-tuple-element.220, s32[]{:T(128)} %get-tuple-element.207), kind=kOutput, calls=%fused_computation.9.clone.1 | convolution fusion | flops 203685376 | bytes 4852272 | tf_op jit(solution)/shard_map/while/body/eval_jaxpr/bhid,bwhkd->bhiwk/dot_general | solution.py:59
  211.2 2.0 gather_fusion
  213.8 3.4 %gather_fusion.3 = bf16[48,128,128]{2,1,0:T(8,128)(2,1)} fusion(bf16[32,128,128]{2,1,0:T(8,128)(2,1)} %bitcast.123, s32[1024]{0:T(1024)S(1)} %pad_clamp_fusion.6), kind=kCustom, calls=%fused_computation.3.clone.1 | custom fusion | bytes 3145920 | tf_op jit(solution)/shard_map/while/body/eval_jaxpr/gather | solution.py:57
  217.2 3.2 %fusion.70 = bf16[8,4,128,1,128]{4,2,1,3,0:T(8,128)(2,1)} fusion(bf16[8,4,128,1,128]{4,2,1,3,0:T(8,128)(2,1)} %get-tuple-element.208, s32[]{:T(128)} %get-tuple-element.207, f32[4,128,128]{2,1,0:T(8,128)S(1)} %convolution_bitcast_fusion.2, bf16[4,12,128,128]{3,2,1,0:T(8,128)(2,1)} %bitcast.124, f32[4,128,12,128]{1,3,2,0:T(8,128)S(1)} %copy-done.2, ...), kind=kOutput, calls=%fused_computation.24.clone.1 | convolution fusion | flops 205455360 | bytes 5116464 | tf_op jit(solution)/shard_map/while/body/eval_jaxpr/bhiwk,bwhkd->bhid/dot_general | solution.py:74
  220.5 2.1 gather_fusion.2
  222.7 3.1 %fusion.67 = (f32[4,128]{1,0:T(4,128)S(1)}, f32[4,128,12,128]{1,3,2,0:T(8,128)}) fusion(pred[4,12]{1,0:T(4,128)(4,1)S(1)} %iota_compare_fusion.2, bf16[4,12,128,128]{3,2,1,0:T(8,128)(2,1)S(1)} %bitcast.120, bf16[8,4,1,128,128]{3,4,1,0,2:T(8,128)(2,1)} %get-tuple-element.220, s32[]{:T(128)} %get-tuple-element.207), kind=kOutput, calls=%fused_computation.9.clone.1 | convolution fusion | flops 203685376 | bytes 4852272 | tf_op jit(solution)/shard_map/while/body/eval_jaxpr/bhid,bwhkd->bhiwk/dot_general | solution.py:59
  233.8 3.4 %gather_fusion.3 = bf16[48,128,128]{2,1,0:T(8,128)(2,1)} fusion(bf16[32,128,128]{2,1,0:T(8,128)(2,1)} %bitcast.123, s32[1024]{0:T(1024)S(1)} %pad_clamp_fusion.6), kind=kCustom, calls=%fused_computation.3.clone.1 | custom fusion | bytes 3145920 | tf_op jit(solution)/shard_map/while/body/eval_jaxpr/gather | solution.py:57
  237.2 3.2 %fusion.70 = bf16[8,4,128,1,128]{4,2,1,3,0:T(8,128)(2,1)} fusion(bf16[8,4,128,1,128]{4,2,1,3,0:T(8,128)(2,1)} %get-tuple-element.208, s32[]{:T(128)} %get-tuple-element.207, f32[4,128,128]{2,1,0:T(8,128)S(1)} %convolution_bitcast_fusion.2, bf16[4,12,128,128]{3,2,1,0:T(8,128)(2,1)} %bitcast.124, f32[4,128,12,128]{1,3,2,0:T(8,128)S(1)} %copy-done.2, ...), kind=kOutput, calls=%fused_computation.24.clone.1 | convolution fusion | flops 205455360 | bytes 5116464 | tf_op jit(solution)/shard_map/while/body/eval_jaxpr/bhiwk,bwhkd->bhid/dot_general | solution.py:74
  240.5 2.1 gather_fusion.2
  242.7 3.1 %fusion.67 = (f32[4,128]{1,0:T(4,128)S(1)}, f32[4,128,12,128]{1,3,2,0:T(8,128)}) fusion(pred[4,12]{1,0:T(4,128)(4,1)S(1)} %iota_compare_fusion.2, bf16[4,12,128,128]{3,2,1,0:T(8,128)(2,1)S(1)} %bitcast.120, bf16[8,4,1,128,128]{3,4,1,0,2:T(8,128)(2,1)} %get-tuple-element.220, s32[]{:T(128)} %get-tuple-element.207), kind=kOutput, calls=%fused_computation.9.clone.1 | convolution fusion | flops 203685376 | bytes 4852272 | tf_op jit(solution)/shard_map/while/body/eval_jaxpr/bhid,bwhkd->bhiwk/dot_general | solution.py:59
  251.2 2.0 gather_fusion
  253.8 3.4 %gather_fusion.3 = bf16[48,128,128]{2,1,0:T(8,128)(2,1)} fusion(bf16[32,128,128]{2,1,0:T(8,128)(2,1)} %bitcast.123, s32[1024]{0:T(1024)S(1)} %pad_clamp_fusion.6), kind=kCustom, calls=%fused_computation.3.clone.1 | custom fusion | bytes 3145920 | tf_op jit(solution)/shard_map/while/body/eval_jaxpr/gather | solution.py:57
  257.2 3.2 %fusion.70 = bf16[8,4,128,1,128]{4,2,1,3,0:T(8,128)(2,1)} fusion(bf16[8,4,128,1,128]{4,2,1,3,0:T(8,128)(2,1)} %get-tuple-element.208, s32[]{:T(128)} %get-tuple-element.207, f32[4,128,128]{2,1,0:T(8,128)S(1)} %convolution_bitcast_fusion.2, bf16[4,12,128,128]{3,2,1,0:T(8,128)(2,1)} %bitcast.124, f32[4,128,12,128]{1,3,2,0:T(8,128)S(1)} %copy-done.2, ...), kind=kOutput, calls=%fused_computation.24.clone.1 | convolution fusion | flops 205455360 | bytes 5116464 | tf_op jit(solution)/shard_map/while/body/eval_jaxpr/bhiwk,bwhkd->bhid/dot_general | solution.py:74
  261.0 2.7 reduce.8
  264.0 34.9 %all_to_all.27 = bf16[32,2,8192]{2,1,0:T(2,128)(2,1)S(1)} all-to-all(bf16[32,2,8192]{2,1,0:T(2,128)(2,1)S(1)} %reshape.276), channel_id=1, replica_groups=mesh['seq'=32,'blk'=8] {'seq'}, dimensions={0} | all-to-all | bytes 2097152 | tf_op jit(solution)/shard_map/all_to_all | solution.py:93
  (185 shorter events, 62.8 us)
Async XLA Ops:
  6.5 19.4 %copy-start = (s32[256]{0:T(256)S(1)}, s32[256]{0:T(256)}, u32[]{:S(2)}) copy-start(s32[256]{0:T(256)} %param.11) | copy-start | bytes 3076
  11.9 11.8 %copy-start.4 = (bf16[4,2,128,128]{3,2,1,0:T(8,128)(2,1)S(1)}, bf16[4,2,128,128]{3,2,1,0:T(8,128)(2,1)}, u32[]{:S(2)}) copy-start(bf16[4,2,128,128]{3,2,1,0:T(8,128)(2,1)} %param.8) | copy-start | bytes 786436
  11.9 12.6 %copy-start.6 = (s32[256,8]{0,1:T(8,128)S(1)}, s32[256,8]{0,1:T(8,128)}, u32[]{:S(2)}) copy-start(s32[256,8]{0,1:T(8,128)} %param.9) | copy-start | bytes 24580
  11.9 12.7 %copy-start.5 = (s32[256,12]{0,1:T(8,128)S(1)}, s32[256,12]{0,1:T(8,128)}, u32[]{:S(2)}) copy-start(s32[256,12]{0,1:T(8,128)} %param.10) | copy-start | bytes 36868
  11.9 83.0 %all-to-all-start = ((bf16[128,3,32,128]{0,3,1,2:T(8,128)(2,1)}), bf16[128,3,32,128]{0,3,1,2:T(8,128)(2,1)S(1)}, u32[]{:S(2)}, u32[]{:S(2)}) async-start(bf16[128,3,32,128]{0,3,1,2:T(8,128)(2,1)} %copy.46), calls=%async_computation | async-start | bytes 6291456 | tf_op jit(solution)/shard_map/all_to_all | solution.py:20
  23.7 31.7 %all-gather.2.cloned.1.call-start = ((), (), s32[]{:S(2)}) async-start(), calls=%async_computation.2 | async-start | bytes 2359296 | tf_op jit(solution)/shard_map/all_gather | solution.py:28
  96.7 2.3 copy-start.3
  107.8 2.0 copy-start.1
  113.7 3.4 %copy-start.2 = (f32[4,128,12,128]{1,3,2,0:T(8,128)S(1)}, f32[4,128,12,128]{1,3,2,0:T(8,128)}, u32[]{:S(2)}) copy-start(f32[4,128,12,128]{1,3,2,0:T(8,128)} %get-tuple-element.195) | copy-start | bytes 9437188 | tf_op jit(solution)/shard_map/while
  127.8 2.0 copy-start.1
  133.7 3.4 %copy-start.2 = (f32[4,128,12,128]{1,3,2,0:T(8,128)S(1)}, f32[4,128,12,128]{1,3,2,0:T(8,128)}, u32[]{:S(2)}) copy-start(f32[4,128,12,128]{1,3,2,0:T(8,128)} %get-tuple-element.195) | copy-start | bytes 9437188 | tf_op jit(solution)/shard_map/while
  147.8 2.0 copy-start.1
  153.7 3.4 %copy-start.2 = (f32[4,128,12,128]{1,3,2,0:T(8,128)S(1)}, f32[4,128,12,128]{1,3,2,0:T(8,128)}, u32[]{:S(2)}) copy-start(f32[4,128,12,128]{1,3,2,0:T(8,128)} %get-tuple-element.195) | copy-start | bytes 9437188 | tf_op jit(solution)/shard_map/while
  167.9 2.0 copy-start.1
  173.7 3.4 %copy-start.2 = (f32[4,128,12,128]{1,3,2,0:T(8,128)S(1)}, f32[4,128,12,128]{1,3,2,0:T(8,128)}, u32[]{:S(2)}) copy-start(f32[4,128,12,128]{1,3,2,0:T(8,128)} %get-tuple-element.195) | copy-start | bytes 9437188 | tf_op jit(solution)/shard_map/while
  187.9 2.0 copy-start.1
  193.8 3.4 %copy-start.2 = (f32[4,128,12,128]{1,3,2,0:T(8,128)S(1)}, f32[4,128,12,128]{1,3,2,0:T(8,128)}, u32[]{:S(2)}) copy-start(f32[4,128,12,128]{1,3,2,0:T(8,128)} %get-tuple-element.195) | copy-start | bytes 9437188 | tf_op jit(solution)/shard_map/while
  207.9 2.0 copy-start.1
  213.8 3.4 %copy-start.2 = (f32[4,128,12,128]{1,3,2,0:T(8,128)S(1)}, f32[4,128,12,128]{1,3,2,0:T(8,128)}, u32[]{:S(2)}) copy-start(f32[4,128,12,128]{1,3,2,0:T(8,128)} %get-tuple-element.195) | copy-start | bytes 9437188 | tf_op jit(solution)/shard_map/while
  227.9 2.0 copy-start.1
  233.8 3.4 %copy-start.2 = (f32[4,128,12,128]{1,3,2,0:T(8,128)S(1)}, f32[4,128,12,128]{1,3,2,0:T(8,128)}, u32[]{:S(2)}) copy-start(f32[4,128,12,128]{1,3,2,0:T(8,128)} %get-tuple-element.195) | copy-start | bytes 9437188 | tf_op jit(solution)/shard_map/while
  247.9 2.0 copy-start.1
  253.8 3.4 %copy-start.2 = (f32[4,128,12,128]{1,3,2,0:T(8,128)S(1)}, f32[4,128,12,128]{1,3,2,0:T(8,128)}, u32[]{:S(2)}) copy-start(f32[4,128,12,128]{1,3,2,0:T(8,128)} %get-tuple-element.195) | copy-start | bytes 9437188 | tf_op jit(solution)/shard_map/while
Sparse Core Ops, SparseCore 0:
  26.3 28.9 all-gather.1
where the time goes:
time: 311 us; the launch traced here: 309 us
  local copies, waits for them, and re-layouts  101 us (32%)
  matrix products  67.9 us (22%)
  waiting for transfers between devices  65.1 us (21%)
  blocking collectives  34.9 us (11%)
  other arithmetic  13.9 us (4%)
  between operations  13.5 us (4%)
  starting transfers between devices  11.8 us (4%)
    all_to_all x1, waiting for transfers between devices, per_device(): lax.all_to_all(shaped, 'seq', split_axis=2, concat_axis=0, tiled=True)  36.5 us
    all_to_all x1, blocking collectives, per_device(): lax.all_to_all(attended, 'seq', split_axis=0, concat_axis=1, tiled=True)  34.9 us
    all_gather x1, waiting for transfers between devices, per_device(): kept_all = lax.all_gather(kept_kv, 'blk', axis=0, tiled=True)  28.6 us
    gather x8, local copies, waits for them, and re-layouts, attend(): far_values = far_values_all[kept_sel]  27.3 us
    dot_general x8, matrix products, attend(): jnp.einsum('bhiwk,bwhkd->bhid', far_weights.astype(jnp.bfloat16), far_val...  25.9 us
    dot_general x8, matrix products, attend(): jnp.einsum('bhid,bwhkd->bhiwk', queries, far_keys, preferred_element_type...  25.1 us
    gather x8, local copies, waits for them, and re-layouts, attend(): far_keys = far_keys_all[kept_sel]  16.6 us
    gather x8, local copies, waits for them, and re-layouts, attend(): near_values = near_values_all[cur_sel]  15.8 us
  transfers between devices with their start and end apart: 2, of which 2 were waited for; matrix products, arithmetic and copies ran while one was open for 2% of the time, Pallas kernels for 0%

commit v1 on v0

--- a/solution.py
+++ b/solution.py
@@ -25,7 +25,9 @@
     queries_all = ordered[0]
     near_keys_all = ordered[1]
     near_values_all = ordered[2]
-    kept_all = lax.all_gather(kept_kv, "blk", axis=0, tiled=True)
+    kept_all = jnp.concatenate(
+        lax.all_to_all(jnp.stack([kept_kv] * lax.axis_size("blk")), "blk", 0, 0), axis=0
+    )
     kept_all = jnp.transpose(
         kept_all.reshape(kept_all.shape[0], 2, tile_len, head_dev, head_width), (0, 1, 3, 2, 4)
     )

time: 311 us -> 325 us (1.045)
  waiting for transfers between devices: 65.1 us -> 87.2 us
  between operations: 13.5 us -> 0.13 us
  starting transfers between devices: 11.8 us -> 16.1 us
    all_to_all x1, waiting for transfers between devices: 36.5 us -> 65.3 us  [per_device(): lax.all_to_all(shaped, 'seq', split_axis=2, concat_axis=0, tiled=True)]
    all_gather x1 -> x0, waiting for transfers between devices: 28.6 us -> none  [per_device(): kept_all = lax.all_gather(kept_kv, 'blk', axis=0, tiled=True)]
    all_to_all x0 -> x1, waiting for transfers between devices: none -> 21.9 us  [per_device(): lax.all_to_all(jnp.stack([kept_kv] * lax.axis_size('blk')), 'blk', 0, 0)]
    all_to_all x0 -> x1, starting transfers between devices: none -> 4.47 us  [per_device(): lax.all_to_all(jnp.stack([kept_kv] * lax.axis_size('blk')), 'blk', 0, 0)]
  transfers between devices with their start and end apart: 2 -> 2, of which waited for: 2 -> 2; matrix products, arithmetic and copies ran while one was open for 2% -> 3% of each run, Pallas kernels for 0% -> 0%
where the time goes in v1:
time: 325 us; the launch traced here: 323 us
  local copies, waits for them, and re-layouts  103 us (32%)
  waiting for transfers between devices  87.2 us (27%)
  matrix products  68 us (21%)
  blocking collectives  34.5 us (11%)
  starting transfers between devices  16.1 us (5%)
  other arithmetic  13.9 us (4%)
    all_to_all x1, waiting for transfers between devices, per_device(): lax.all_to_all(shaped, 'seq', split_axis=2, concat_axis=0, tiled=True)  65.3 us
    all_to_all x1, blocking collectives, per_device(): lax.all_to_all(attended, 'seq', split_axis=0, concat_axis=1, tiled=True)  34.5 us
    gather x8, local copies, waits for them, and re-layouts, attend(): far_values = far_values_all[kept_sel]  26.6 us
    dot_general x8, matrix products, attend(): jnp.einsum('bhiwk,bwhkd->bhid', far_weights.astype(jnp.bfloat16), far_val...  25.9 us
    dot_general x8, matrix products, attend(): jnp.einsum('bhid,bwhkd->bhiwk', queries, far_keys, preferred_element_type...  25.2 us
    all_to_all x1, waiting for transfers between devices, per_device(): lax.all_to_all(jnp.stack([kept_kv] * lax.axis_size('blk')), 'blk', 0, 0)  21.9 us
    gather x8, local copies, waits for them, and re-layouts, attend(): far_keys = far_keys_all[kept_sel]  16.6 us
    gather x8, local copies, waits for them, and re-layouts, attend(): near_values = near_values_all[cur_sel]  15.8 us
  transfers between devices with their start and end apart: 2, of which 2 were waited for; matrix products, arithmetic and copies ran while one was open for 3% of the time, Pallas kernels for 0%

profile of v1, /device:TPU:2, one launch (start us, length us, event | category | flops | bytes accessed | tf_op | source)
XLA Modules:
  0.0 323.1 jit_solution(12953275607247200835)
XLA Ops:
  2.9 4.5 %all-to-all-start.1 = ((bf16[8,4,2,128,128]{4,3,1,2,0:T(8,128)(2,1)}), bf16[8,4,2,128,128]{4,3,1,2,0:T(8,128)(2,1)}, u32[]{:S(2)}, u32[]{:S(2)}) async-start(bf16[8,4,2,128,128]{4,3,1,2,0:T(8,128)(2,1)} %stack.2), calls=%async_computation.1 | async-start | bytes 4194304 | tf_op jit(solution)/shard_map/all_to_all | solution.py:29
  7.3 3.5 %copy.45 = bf16[128,12288]{0,1:T(8,128)(2,1)S(1)} copy(bf16[128,12288]{1,0:T(8,128)(2,1)} %param.7) | data formatting | bytes 6291456 | tf_op args[0]
  12.7 21.9 %all-to-all-done.1 = bf16[8,4,2,128,128]{4,3,1,2,0:T(8,128)(2,1)} async-done(((bf16[8,4,2,128,128]{4,3,1,2,0:T(8,128)(2,1)}), bf16[8,4,2,128,128]{4,3,1,2,0:T(8,128)(2,1)}, u32[]{:S(2)}, u32[]{:S(2)}) %all-to-all-start.1) | async-done | bytes 2097184 | tf_op jit(solution)/shard_map/all_to_all | solution.py:29
  34.6 11.6 %all-to-all-start = ((bf16[128,3,32,128]{0,3,1,2:T(8,128)(2,1)}), bf16[128,3,32,128]{0,3,1,2:T(8,128)(2,1)S(1)}, u32[]{:S(2)}, u32[]{:S(2)}) async-start(bf16[128,3,32,128]{0,3,1,2:T(8,128)(2,1)} %copy.46), calls=%async_computation | async-start | bytes 6291456 | tf_op jit(solution)/shard_map/all_to_all | solution.py:20
  51.7 65.3 %all-to-all-done = bf16[128,3,32,128]{0,3,1,2:T(8,128)(2,1)S(1)} async-done(((bf16[128,3,32,128]{0,3,1,2:T(8,128)(2,1)}), bf16[128,3,32,128]{0,3,1,2:T(8,128)(2,1)S(1)}, u32[]{:S(2)}, u32[]{:S(2)}) %all-to-all-start) | async-done | bytes 3145760 | tf_op jit(solution)/shard_map/all_to_all | solution.py:20
  118.7 2.4 copy.52
  122.5 159.6 %while.10 = (s32[]{:T(128)}, bf16[8,4,128,1,128]{4,2,1,3,0:T(8,128)(2,1)}, bf16[8,4,1,128,128]{3,4,1,0,2:T(8,128)(2,1)}, s32[8,4,8]{2,1,0:T(4,128)S(1)}, bf16[32...) while((s32[]{:T(128)}, ...), condition=%wide.region_5.6_spmd, body=%wide.region_0.5_spmd.sunk | while | flops 685704448 | bytes 57583712 | solution.py:85
  122.6 2.1 gather_fusion.2
  124.7 3.1 fusion.67
  133.2 2.0 gather_fusion
  135.9 3.3 %gather_fusion.3 = bf16[48,128,128]{2,1,0:T(8,128)(2,1)} fusion(bf16[32,128,128]{2,1,0:T(8,128)(2,1)} %bitcast.127, s32[1024]{0:T(1024)S(1)} %pad_clamp_fusion.6), kind=kCustom, calls=%fused_computation.3.clone.1 | custom fusion | bytes 3145920 | tf_op jit(solution)/shard_map/while/body/eval_jaxpr/gather | solution.py:59
  139.2 3.2 %fusion.70 = bf16[8,4,128,1,128]{4,2,1,3,0:T(8,128)(2,1)} fusion(bf16[8,4,128,1,128]{4,2,1,3,0:T(8,128)(2,1)} %get-tuple-element.208, s32[]{:T(128)} %get-tuple-element.207, f32[4,128,128]{2,1,0:T(8,128)S(1)} %convolution_bitcast_fusion.2, bf16[4,12,128,128]{3,2,1,0:T(8,128)(2,1)} %bitcast.128, f32[4,128,12,128]{1,3,2,0:T(8,128)S(1)} %copy-done.2, ...), kind=kOutput, calls=%fused_computation.24.clone.1 | convolution fusion | flops 205455360 | bytes 5116464 | tf_op jit(solution)/shard_map/while/body/eval_jaxpr/bhiwk,bwhkd->bhid/dot_general | solution.py:76
  142.5 2.1 gather_fusion.2
  144.7 3.1 fusion.67
  153.2 2.0 gather_fusion
  155.8 3.3 %gather_fusion.3 = bf16[48,128,128]{2,1,0:T(8,128)(2,1)} fusion(bf16[32,128,128]{2,1,0:T(8,128)(2,1)} %bitcast.127, s32[1024]{0:T(1024)S(1)} %pad_clamp_fusion.6), kind=kCustom, calls=%fused_computation.3.clone.1 | custom fusion | bytes 3145920 | tf_op jit(solution)/shard_map/while/body/eval_jaxpr/gather | solution.py:59
  159.1 3.2 %fusion.70 = bf16[8,4,128,1,128]{4,2,1,3,0:T(8,128)(2,1)} fusion(bf16[8,4,128,1,128]{4,2,1,3,0:T(8,128)(2,1)} %get-tuple-element.208, s32[]{:T(128)} %get-tuple-element.207, f32[4,128,128]{2,1,0:T(8,128)S(1)} %convolution_bitcast_fusion.2, bf16[4,12,128,128]{3,2,1,0:T(8,128)(2,1)} %bitcast.128, f32[4,128,12,128]{1,3,2,0:T(8,128)S(1)} %copy-done.2, ...), kind=kOutput, calls=%fused_computation.24.clone.1 | convolution fusion | flops 205455360 | bytes 5116464 | tf_op jit(solution)/shard_map/while/body/eval_jaxpr/bhiwk,bwhkd->bhid/dot_general | solution.py:76
  162.5 2.1 gather_fusion.2
  164.6 3.1 fusion.67
  173.1 2.0 gather_fusion
  175.8 3.3 %gather_fusion.3 = bf16[48,128,128]{2,1,0:T(8,128)(2,1)} fusion(bf16[32,128,128]{2,1,0:T(8,128)(2,1)} %bitcast.127, s32[1024]{0:T(1024)S(1)} %pad_clamp_fusion.6), kind=kCustom, calls=%fused_computation.3.clone.1 | custom fusion | bytes 3145920 | tf_op jit(solution)/shard_map/while/body/eval_jaxpr/gather | solution.py:59
  179.1 3.2 %fusion.70 = bf16[8,4,128,1,128]{4,2,1,3,0:T(8,128)(2,1)} fusion(bf16[8,4,128,1,128]{4,2,1,3,0:T(8,128)(2,1)} %get-tuple-element.208, s32[]{:T(128)} %get-tuple-element.207, f32[4,128,128]{2,1,0:T(8,128)S(1)} %convolution_bitcast_fusion.2, bf16[4,12,128,128]{3,2,1,0:T(8,128)(2,1)} %bitcast.128, f32[4,128,12,128]{1,3,2,0:T(8,128)S(1)} %copy-done.2, ...), kind=kOutput, calls=%fused_computation.24.clone.1 | convolution fusion | flops 205455360 | bytes 5116464 | tf_op jit(solution)/shard_map/while/body/eval_jaxpr/bhiwk,bwhkd->bhid/dot_general | solution.py:76
  182.4 2.1 gather_fusion.2
  184.6 3.1 fusion.67
  193.1 2.0 gather_fusion
  195.7 3.3 %gather_fusion.3 = bf16[48,128,128]{2,1,0:T(8,128)(2,1)} fusion(bf16[32,128,128]{2,1,0:T(8,128)(2,1)} %bitcast.127, s32[1024]{0:T(1024)S(1)} %pad_clamp_fusion.6), kind=kCustom, calls=%fused_computation.3.clone.1 | custom fusion | bytes 3145920 | tf_op jit(solution)/shard_map/while/body/eval_jaxpr/gather | solution.py:59
  199.0 3.2 %fusion.70 = bf16[8,4,128,1,128]{4,2,1,3,0:T(8,128)(2,1)} fusion(bf16[8,4,128,1,128]{4,2,1,3,0:T(8,128)(2,1)} %get-tuple-element.208, s32[]{:T(128)} %get-tuple-element.207, f32[4,128,128]{2,1,0:T(8,128)S(1)} %convolution_bitcast_fusion.2, bf16[4,12,128,128]{3,2,1,0:T(8,128)(2,1)} %bitcast.128, f32[4,128,12,128]{1,3,2,0:T(8,128)S(1)} %copy-done.2, ...), kind=kOutput, calls=%fused_computation.24.clone.1 | convolution fusion | flops 205455360 | bytes 5116464 | tf_op jit(solution)/shard_map/while/body/eval_jaxpr/bhiwk,bwhkd->bhid/dot_general | solution.py:76
  202.4 2.1 gather_fusion.2
  204.5 3.1 fusion.67
  213.0 2.0 gather_fusion
  215.7 3.3 %gather_fusion.3 = bf16[48,128,128]{2,1,0:T(8,128)(2,1)} fusion(bf16[32,128,128]{2,1,0:T(8,128)(2,1)} %bitcast.127, s32[1024]{0:T(1024)S(1)} %pad_clamp_fusion.6), kind=kCustom, calls=%fused_computation.3.clone.1 | custom fusion | bytes 3145920 | tf_op jit(solution)/shard_map/while/body/eval_jaxpr/gather | solution.py:59
  219.0 3.2 %fusion.70 = bf16[8,4,128,1,128]{4,2,1,3,0:T(8,128)(2,1)} fusion(bf16[8,4,128,1,128]{4,2,1,3,0:T(8,128)(2,1)} %get-tuple-element.208, s32[]{:T(128)} %get-tuple-element.207, f32[4,128,128]{2,1,0:T(8,128)S(1)} %convolution_bitcast_fusion.2, bf16[4,12,128,128]{3,2,1,0:T(8,128)(2,1)} %bitcast.128, f32[4,128,12,128]{1,3,2,0:T(8,128)S(1)} %copy-done.2, ...), kind=kOutput, calls=%fused_computation.24.clone.1 | convolution fusion | flops 205455360 | bytes 5116464 | tf_op jit(solution)/shard_map/while/body/eval_jaxpr/bhiwk,bwhkd->bhid/dot_general | solution.py:76
  222.3 2.1 gather_fusion.2
  224.5 3.1 fusion.67
  233.0 2.0 gather_fusion
  235.6 3.3 %gather_fusion.3 = bf16[48,128,128]{2,1,0:T(8,128)(2,1)} fusion(bf16[32,128,128]{2,1,0:T(8,128)(2,1)} %bitcast.127, s32[1024]{0:T(1024)S(1)} %pad_clamp_fusion.6), kind=kCustom, calls=%fused_computation.3.clone.1 | custom fusion | bytes 3145920 | tf_op jit(solution)/shard_map/while/body/eval_jaxpr/gather | solution.py:59
  238.9 3.2 %fusion.70 = bf16[8,4,128,1,128]{4,2,1,3,0:T(8,128)(2,1)} fusion(bf16[8,4,128,1,128]{4,2,1,3,0:T(8,128)(2,1)} %get-tuple-element.208, s32[]{:T(128)} %get-tuple-element.207, f32[4,128,128]{2,1,0:T(8,128)S(1)} %convolution_bitcast_fusion.2, bf16[4,12,128,128]{3,2,1,0:T(8,128)(2,1)} %bitcast.128, f32[4,128,12,128]{1,3,2,0:T(8,128)S(1)} %copy-done.2, ...), kind=kOutput, calls=%fused_computation.24.clone.1 | convolution fusion | flops 205455360 | bytes 5116464 | tf_op jit(solution)/shard_map/while/body/eval_jaxpr/bhiwk,bwhkd->bhid/dot_general | solution.py:76
  242.3 2.1 gather_fusion.2
  244.4 3.1 fusion.67
  252.9 2.0 gather_fusion
  255.6 3.3 %gather_fusion.3 = bf16[48,128,128]{2,1,0:T(8,128)(2,1)} fusion(bf16[32,128,128]{2,1,0:T(8,128)(2,1)} %bitcast.127, s32[1024]{0:T(1024)S(1)} %pad_clamp_fusion.6), kind=kCustom, calls=%fused_computation.3.clone.1 | custom fusion | bytes 3145920 | tf_op jit(solution)/shard_map/while/body/eval_jaxpr/gather | solution.py:59
  258.9 3.2 %fusion.70 = bf16[8,4,128,1,128]{4,2,1,3,0:T(8,128)(2,1)} fusion(bf16[8,4,128,1,128]{4,2,1,3,0:T(8,128)(2,1)} %get-tuple-element.208, s32[]{:T(128)} %get-tuple-element.207, f32[4,128,128]{2,1,0:T(8,128)S(1)} %convolution_bitcast_fusion.2, bf16[4,12,128,128]{3,2,1,0:T(8,128)(2,1)} %bitcast.128, f32[4,128,12,128]{1,3,2,0:T(8,128)S(1)} %copy-done.2, ...), kind=kOutput, calls=%fused_computation.24.clone.1 | convolution fusion | flops 205455360 | bytes 5116464 | tf_op jit(solution)/shard_map/while/body/eval_jaxpr/bhiwk,bwhkd->bhid/dot_general | solution.py:76
  262.2 2.1 gather_fusion.2
  264.4 3.1 fusion.67
  275.5 3.3 %gather_fusion.3 = bf16[48,128,128]{2,1,0:T(8,128)(2,1)} fusion(bf16[32,128,128]{2,1,0:T(8,128)(2,1)} %bitcast.127, s32[1024]{0:T(1024)S(1)} %pad_clamp_fusion.6), kind=kCustom, calls=%fused_computation.3.clone.1 | custom fusion | bytes 3145920 | tf_op jit(solution)/shard_map/while/body/eval_jaxpr/gather | solution.py:59
  278.8 3.2 %fusion.70 = bf16[8,4,128,1,128]{4,2,1,3,0:T(8,128)(2,1)} fusion(bf16[8,4,128,1,128]{4,2,1,3,0:T(8,128)(2,1)} %get-tuple-element.208, s32[]{:T(128)} %get-tuple-element.207, f32[4,128,128]{2,1,0:T(8,128)S(1)} %convolution_bitcast_fusion.2, bf16[4,12,128,128]{3,2,1,0:T(8,128)(2,1)} %bitcast.128, f32[4,128,12,128]{1,3,2,0:T(8,128)S(1)} %copy-done.2, ...), kind=kOutput, calls=%fused_computation.24.clone.1 | convolution fusion | flops 205455360 | bytes 5116464 | tf_op jit(solution)/shard_map/while/body/eval_jaxpr/bhiwk,bwhkd->bhid/dot_general | solution.py:76
  282.6 2.6 reduce.8
  285.4 34.5 %all_to_all.32 = bf16[32,2,8192]{2,1,0:T(2,128)(2,1)S(1)} all-to-all(bf16[32,2,8192]{2,1,0:T(2,128)(2,1)S(1)} %reshape.278), channel_id=1, replica_groups=mesh['seq'=32,'blk'=8] {'seq'}, dimensions={0} | all-to-all | bytes 2097152 | tf_op jit(solution)/shard_map/all_to_all | solution.py:95
  (184 shorter events, 68.0 us)
Async XLA Ops:
  0.0 47.7 %copy-start = (s32[256]{0:T(256)S(1)}, s32[256]{0:T(256)}, u32[]{:S(2)}) copy-start(s32[256]{0:T(256)} %param.11) | copy-start | bytes 3076
  2.9 31.7 %all-to-all-start.1 = ((bf16[8,4,2,128,128]{4,3,1,2,0:T(8,128)(2,1)}), bf16[8,4,2,128,128]{4,3,1,2,0:T(8,128)(2,1)}, u32[]{:S(2)}, u32[]{:S(2)}) async-start(bf16[8,4,2,128,128]{4,3,1,2,0:T(8,128)(2,1)} %stack.2), calls=%async_computation.1 | async-start | bytes 4194304 | tf_op jit(solution)/shard_map/all_to_all | solution.py:29
  12.7 33.5 %copy-start.5 = (s32[256,8]{0,1:T(8,128)S(1)}, s32[256,8]{0,1:T(8,128)}, u32[]{:S(2)}) copy-start(s32[256,8]{0,1:T(8,128)} %param.9) | copy-start | bytes 24580
  12.7 33.7 %copy-start.4 = (s32[256,12]{0,1:T(8,128)S(1)}, s32[256,12]{0,1:T(8,128)}, u32[]{:S(2)}) copy-start(s32[256,12]{0,1:T(8,128)} %param.10) | copy-start | bytes 36868
  34.6 82.4 %all-to-all-start = ((bf16[128,3,32,128]{0,3,1,2:T(8,128)(2,1)}), bf16[128,3,32,128]{0,3,1,2:T(8,128)(2,1)S(1)}, u32[]{:S(2)}, u32[]{:S(2)}) async-start(bf16[128,3,32,128]{0,3,1,2:T(8,128)(2,1)} %copy.46), calls=%async_computation | async-start | bytes 6291456 | tf_op jit(solution)/shard_map/all_to_all | solution.py:20
  118.7 2.4 copy-start.3
  130.0 2.0 copy-start.1
  135.8 3.3 %copy-start.2 = (f32[4,128,12,128]{1,3,2,0:T(8,128)S(1)}, f32[4,128,12,128]{1,3,2,0:T(8,128)}, u32[]{:S(2)}) copy-start(f32[4,128,12,128]{1,3,2,0:T(8,128)} %get-tuple-element.195) | copy-start | bytes 9437188 | tf_op jit(solution)/shard_map/while
  149.9 2.0 copy-start.1
  155.8 3.3 %copy-start.2 = (f32[4,128,12,128]{1,3,2,0:T(8,128)S(1)}, f32[4,128,12,128]{1,3,2,0:T(8,128)}, u32[]{:S(2)}) copy-start(f32[4,128,12,128]{1,3,2,0:T(8,128)} %get-tuple-element.195) | copy-start | bytes 9437188 | tf_op jit(solution)/shard_map/while
  169.9 2.0 copy-start.1
  175.7 3.3 %copy-start.2 = (f32[4,128,12,128]{1,3,2,0:T(8,128)S(1)}, f32[4,128,12,128]{1,3,2,0:T(8,128)}, u32[]{:S(2)}) copy-start(f32[4,128,12,128]{1,3,2,0:T(8,128)} %get-tuple-element.195) | copy-start | bytes 9437188 | tf_op jit(solution)/shard_map/while
  189.8 2.0 copy-start.1
  195.7 3.3 %copy-start.2 = (f32[4,128,12,128]{1,3,2,0:T(8,128)S(1)}, f32[4,128,12,128]{1,3,2,0:T(8,128)}, u32[]{:S(2)}) copy-start(f32[4,128,12,128]{1,3,2,0:T(8,128)} %get-tuple-element.195) | copy-start | bytes 9437188 | tf_op jit(solution)/shard_map/while
  209.8 2.0 copy-start.1
  215.6 3.3 %copy-start.2 = (f32[4,128,12,128]{1,3,2,0:T(8,128)S(1)}, f32[4,128,12,128]{1,3,2,0:T(8,128)}, u32[]{:S(2)}) copy-start(f32[4,128,12,128]{1,3,2,0:T(8,128)} %get-tuple-element.195) | copy-start | bytes 9437188 | tf_op jit(solution)/shard_map/while
  229.7 2.0 copy-start.1
  235.6 3.3 %copy-start.2 = (f32[4,128,12,128]{1,3,2,0:T(8,128)S(1)}, f32[4,128,12,128]{1,3,2,0:T(8,128)}, u32[]{:S(2)}) copy-start(f32[4,128,12,128]{1,3,2,0:T(8,128)} %get-tuple-element.195) | copy-start | bytes 9437188 | tf_op jit(solution)/shard_map/while
  249.7 2.0 copy-start.1
  255.5 3.3 %copy-start.2 = (f32[4,128,12,128]{1,3,2,0:T(8,128)S(1)}, f32[4,128,12,128]{1,3,2,0:T(8,128)}, u32[]{:S(2)}) copy-start(f32[4,128,12,128]{1,3,2,0:T(8,128)} %get-tuple-element.195) | copy-start | bytes 9437188 | tf_op jit(solution)/shard_map/while
  269.6 2.0 copy-start.1
  275.5 3.3 %copy-start.2 = (f32[4,128,12,128]{1,3,2,0:T(8,128)S(1)}, f32[4,128,12,128]{1,3,2,0:T(8,128)}, u32[]{:S(2)}) copy-start(f32[4,128,12,128]{1,3,2,0:T(8,128)} %get-tuple-element.195) | copy-start | bytes 9437188 | tf_op jit(solution)/shard_map/while
